TPU v7x, 512 devices: a whole 4x8x8 slice. The times are simulated.
512 devices in a mesh: member: 8 (over y_lo, core), slab: 64 (over y_hi, x, z).
Axes of the slice: x: 4, y: 8 (y_hi: 2, y_lo: 4; y = y_hi * 4 + y_lo), z: 8, core: 2. Of those that a mesh axis runs over, the one named last changes fastest.
Arguments:
- base_field: bfloat16 [32, 512, 2, 512], P(None, 'slab'), may hold values from -6 to 6
- forcing: bfloat16 [512, 2, 512], P('slab'), may hold values from -6 to 6
- load: float32 [32], replicated, may hold values from 0.25 to 1.75
- amplitudes: float32 [16], replicated, may hold values from 0.25 to 2
- amp_index: int32 [8], P('member'), may hold values from 0 to 15
- mode_count: int32 [8], P('member'), may hold values from 32 to 64, as said below
- point_weight: bfloat16 [32, 32], replicated, may hold values from -1 to 1
- point_bias: float32 [32], replicated, may hold values from -3 to 3
- spectral_weight: bfloat16 [64, 64, 2, 32, 32], P('slab'), may hold values from -6 to 6
Outputs:
- dependence: bfloat16 [32, 512, 2, 512], P('member', 'slab')
Inputs may be any that keep to these rules, and one draw needn't show every extreme that they name: `mode_count`: each member keeps the second-dimension modes below its count; some member keeps all 64.
All inputs are finite; a program needn't handle non-finite values.
Results may differ from a plain program's by a relative error of at most 0.015.
Values may be sent and summed in bfloat16 or wider, within the bound.
A program may use at most 64 MiB of HBM per device.

v0:
```python
import math
import jax
import jax.numpy as jnp
from jax import lax
from jax.sharding import PartitionSpec as P

TWO_PI = 2.0 * math.pi


def phases(frequency, positions, length):
    product = frequency[:, None] * positions[None, :] % length
    angles = product.astype(jnp.float32) * (TWO_PI / length)
    return (jnp.cos(angles), jnp.sin(angles))


def forward_x(pencil, cos_table, sin_table):
    row_total = pencil.shape[0]
    modes = cos_table.shape[0]
    with_cos = jnp.einsum(
        "kxf,mx->kmf", pencil, cos_table, preferred_element_type=jnp.float32
    ).reshape(row_total, modes, 2, -1)
    with_sin = jnp.einsum(
        "kxf,mx->kmf", pencil, sin_table, preferred_element_type=jnp.float32
    ).reshape(row_total, modes, 2, -1)
    real_part = with_cos[:, :, 0] + with_sin[:, :, 1]
    imag_part = with_cos[:, :, 1] - with_sin[:, :, 0]
    return jnp.stack([real_part, imag_part], axis=2).reshape(row_total, modes, -1)


def inverse_x(spectra, cos_table, sin_table):
    row_total = spectra.shape[0]
    points = cos_table.shape[1]
    with_cos = jnp.einsum(
        "kmf,mx->kxf", spectra, cos_table, preferred_element_type=jnp.float32
    ).reshape(row_total, points, 2, -1)
    with_sin = jnp.einsum(
        "kmf,mx->kxf", spectra, sin_table, preferred_element_type=jnp.float32
    ).reshape(row_total, points, 2, -1)
    real_part = with_cos[:, :, 0] - with_sin[:, :, 1]
    imag_part = with_cos[:, :, 1] + with_sin[:, :, 0]
    return jnp.stack([real_part, imag_part], axis=2).reshape(row_total, points, -1)


def mixing(weights, values):
    return jnp.einsum("kmoi,kmiz->kmoz", weights, values, preferred_element_type=jnp.float32)


def local(
    base_field,
    forcing,
    load,
    amplitudes,
    amp_index,
    mode_count,
    point_weight,
    point_bias,
    spectral_weight,
):
    channels, slab_rows, plane_count, length_y = base_field.shape
    slab_count = lax.axis_size("slab")
    local_modes = spectral_weight.shape[0]
    modes_y = local_modes * slab_count
    modes_x = spectral_weight.shape[1]
    length_x = slab_rows * slab_count
    packed_width = 2 * channels * plane_count
    slab_index = lax.axis_index("slab")
    level_ids = jnp.arange(amplitudes.shape[0], dtype=jnp.int32)
    amplitude = jnp.sum(jnp.where(level_ids == amp_index[0], amplitudes, 0.0))
    driven = base_field.astype(jnp.float32) + amplitude * load[:, None, None, None] * forcing[
        None
    ].astype(jnp.float32)
    field_now = (2.0 * jnp.tanh(0.5 * driven)).astype(jnp.bfloat16)
    y_cos, y_sin = phases(
        jnp.arange(modes_y, dtype=jnp.int32), jnp.arange(length_y, dtype=jnp.int32), length_y
    )
    y_real = jnp.einsum(
        "cxzy,ky->kxcz", field_now, y_cos.astype(jnp.bfloat16), preferred_element_type=jnp.float32
    )
    y_imag = -jnp.einsum(
        "cxzy,ky->kxcz", field_now, y_sin.astype(jnp.bfloat16), preferred_element_type=jnp.float32
    )
    packed = (
        jnp.stack([y_real, y_imag], axis=2)
        .astype(jnp.bfloat16)
        .reshape(modes_y, slab_rows, packed_width)
    )
    frequency_x = jnp.concatenate(
        [
            jnp.arange(modes_x // 2, dtype=jnp.int32),
            jnp.arange(length_x - modes_x // 2, length_x, dtype=jnp.int32),
        ]
    )
    local_points = slab_index * slab_rows + jnp.arange(slab_rows, dtype=jnp.int32)
    part_cos, part_sin = phases(frequency_x, local_points, length_x)
    part_cos = part_cos.astype(jnp.bfloat16)
    part_sin = part_sin.astype(jnp.bfloat16)
    full_cos, full_sin = phases(frequency_x, jnp.arange(length_x, dtype=jnp.int32), length_x)
    full_cos = full_cos.astype(jnp.bfloat16)
    full_sin = full_sin.astype(jnp.bfloat16)
    spectrum = lax.psum_scatter(
        forward_x(packed, part_cos, part_sin), "slab", scatter_dimension=0, tiled=True
    )
    spectrum = spectrum.astype(jnp.bfloat16).reshape(local_modes, modes_x, 2, channels, plane_count)
    weight_real = spectral_weight[:, :, 0]
    weight_imag = spectral_weight[:, :, 1]
    spec_real = spectrum[:, :, 0]
    spec_imag = spectrum[:, :, 1]
    mix_real = mixing(weight_real, spec_real) - mixing(weight_imag, spec_imag)
    mix_imag = mixing(weight_real, spec_imag) + mixing(weight_imag, spec_real)
    global_modes = slab_index * local_modes + jnp.arange(local_modes, dtype=jnp.int32)
    keep = (global_modes < mode_count[0]).astype(jnp.float32)[:, None, None, None, None]
    mixed = (
        (jnp.stack([mix_real, mix_imag], axis=2) * keep)
        .astype(jnp.bfloat16)
        .reshape(local_modes, modes_x, packed_width)
    )
    returned = inverse_x(
        lax.all_gather(mixed, "slab", axis=0, tiled=True), part_cos, part_sin
    ).astype(jnp.bfloat16)
    returned = returned.reshape(modes_y, slab_rows, 2, channels, plane_count)
    weights_y = jnp.where(jnp.arange(modes_y) == 0, 1.0, 2.0).astype(jnp.float32) / (
        length_x * length_y
    )
    back_cos = (weights_y[:, None] * y_cos).astype(jnp.bfloat16)
    back_sin = (weights_y[:, None] * y_sin).astype(jnp.bfloat16)
    spectral = jnp.einsum(
        "kxcz,ky->cxzy", returned[:, :, 0], back_cos, preferred_element_type=jnp.float32
    )
    spectral = spectral - jnp.einsum(
        "kxcz,ky->cxzy", returned[:, :, 1], back_sin, preferred_element_type=jnp.float32
    )
    pointwise = (
        jnp.einsum("oc,cxzy->oxzy", point_weight, field_now, preferred_element_type=jnp.float32)
        + point_bias[:, None, None, None]
    )
    layer = jax.nn.gelu(pointwise + spectral, approximate=True).astype(jnp.bfloat16)
    layer = lax.optimization_barrier(layer).astype(jnp.float32)
    total = lax.psum_scatter(
        layer.astype(jnp.bfloat16), "member", scatter_dimension=0, tiled=True
    ).astype(jnp.float32)
    return (total / lax.axis_size("member")).astype(jnp.bfloat16)


def solution(mesh):
    in_specs = (
        P(None, "slab", None, None),
        P("slab", None, None),
        P(),
        P(),
        P("member"),
        P("member"),
        P(),
        P(),
        P("slab", None, None, None, None),
    )
    out_specs = P("member", "slab", None, None)
    return jax.shard_map(local, mesh=mesh, in_specs=in_specs, out_specs=out_specs, check_vma=False)
```

profile of v0, /device:TPU:2, one launch (start us, length us, event | category | flops | bytes accessed | tf_op | source)
XLA Modules:
  0.0 677.5 jit_solution(10603344090468271848)
XLA Ops:
  6.5 0.0 copy-start
  6.5 0.0 reduce-scatter.3.cloned.1.call-start
  6.5 0.7 convert_element_type.81
  7.9 1.3 fusion.62
  9.3 1.3 broadcast_multiply_fusion
  10.5 1.4 multiply_convert_fusion
  12.0 0.8 fusion.4
  12.8 0.8 fusion.5
  13.5 0.1 pad_maximum_fusion.1
  13.6 0.2 copy.52
  13.8 0.2 copy.53
  14.0 0.1 pad_add_fusion
  14.1 1.9 convolution_bitcast_fusion.1
  16.0 0.6 convolution_bitcast_fusion
  16.6 5.8 reshape.104
  22.4 3.7 reshape.105
  26.1 11.8 %slice_add_fusion = (f32[64,64,1,64]{3,2,1,0:T(1,128)S(1)}, f32[64,64,1,64]{3,2,1,0:T(1,128)S(1)}) fusion(f32[64,64,2,64]{3,2,1,0:T(2,128)} %reshape.105, f32[64,64,2,64]{3,2,1,0:T(2,128)} %reshape.104), kind=kLoop, calls=%fused_computation.2 | loop fusion | flops 524288 | bytes 6291456 | tf_op jit(solution)/shard_map/add | solution.py:25
  37.9 6.8 %pad_maximum_fusion = f32[64,64,2,64]{3,2,1,0:T(2,128)} fusion(f32[64,64,1,64]{3,2,1,0:T(1,128)S(1)} %get-tuple-element.6, f32[64,64,1,64]{3,2,1,0:T(1,128)S(1)} %get-tuple-element.5), kind=kLoop, calls=%fused_computation | loop fusion | flops 524288 | bytes 4194304 | tf_op jit(solution)/shard_map/stack | solution.py:27
  44.7 7.2 %copy.55 = f32[64,64,2,64]{1,3,2,0:T(8,128)} copy(f32[64,64,2,64]{3,2,1,0:T(2,128)} %pad_maximum_fusion) | data formatting | bytes 4194304 | tf_op jit(solution)/shard_map/stack | solution.py:27
  51.9 0.0 copy-start.3
  51.9 0.0 reduce-scatter.3.cloned.1.call-update
  52.0 0.3 all-gather.2.cloned.1.call-start
  52.2 0.7 copy-done.3
  53.0 0.8 copy.84
  53.8 0.0 copy-start.4
  53.8 0.8 copy.82
  55.3 422.5 %reduce-scatter.3.cloned.1.call-done = f32[1,64,128]{1,2,0:T(8,128)} async-done(((f32[64,64,128]{1,2,0:T(8,128)}), f32[1,64,128]{1,2,0:T(8,128)}) %reduce-scatter.3.cloned.1.call-update) | async-done | bytes 32784 | tf_op jit(solution)/shard_map/reduce_scatter | solution.py:100
  477.8 0.8 convert_element_type.91
  478.6 0.1 copy.83
  478.7 0.1 copy.81
  478.9 0.4 fusion.16
  479.2 0.4 fusion.14
  479.6 0.4 fusion.20
  480.0 0.4 fusion.18
  480.4 0.1 copy.61
  480.5 0.1 copy.60
  480.5 0.1 copy.63
  480.6 0.1 copy.62
  480.8 0.7 copy.65
  481.5 0.0 all-gather.2.cloned.1.call-update
  481.5 0.0 reduce-scatter.5.cloned.1.call-start
  481.6 0.0 copy-done
  481.6 0.0 copy-done.4
  481.6 1.3 fusion.2
  482.9 148.2 %all-gather.2.cloned.1.call-done = bf16[64,64,128]{2,1,0:T(8,128)(2,1)} async-done(((bf16[1,64,128]{2,1,0:T(8,128)(2,1)}), bf16[64,64,128]{2,1,0:T(8,128)(2,1)}) %all-gather.2.cloned.1.call-update) | async-done | bytes 1048592 | tf_op jit(solution)/shard_map/all_gather | solution.py:118
  631.1 0.0 copy-start.1
  631.1 1.7 convolution_bitcast_fusion.3
  632.8 0.3 copy.79
  633.0 0.0 copy-done.1
  633.0 0.4 convolution_bitcast_fusion.2
  633.4 0.0 copy-start.2
  633.4 0.3 copy.80
  633.7 0.1 fusion.23
  633.7 0.1 pad_maximum_fusion.2
  633.8 0.8 fusion.27
  634.6 0.0 copy-done.2
  634.6 1.0 fusion.13
  635.6 1.1 copy.72
  636.7 0.0 reduce-scatter.5.cloned.1.call-update
  636.7 32.7 %reduce-scatter.5.cloned.1.call-done = bf16[4,8,2,512]{3,1,2,0:T(8,128)(2,1)} async-done(((bf16[32,8,2,512]{3,1,2,0:T(8,128)(2,1)}), bf16[4,8,2,512]{3,1,2,0:T(8,128)(2,1)}) %reduce-scatter.5.cloned.1.call-update) | async-done | bytes 65552 | tf_op jit(solution)/shard_map/reduce_scatter | solution.py:138
  669.5 0.9 multiply_convert_fusion.1
  670.3 0.7 copy.73
  (10 shorter events, 0.2 us)
Async XLA Ops:
  6.5 475.1 %copy-start = (bf16[32,32]{1,0:T(8,128)(2,1)S(1)}, bf16[32,32]{1,0:T(8,128)(2,1)}, u32[]{:S(2)}) copy-start(bf16[32,32]{1,0:T(8,128)(2,1)} %param.15) | copy-start | bytes 6148
  6.5 471.2 %reduce-scatter.3.cloned.1.call-start = ((), (), s32[]{:S(2)}) async-start(), calls=%async_computation.2 | async-start | bytes 4259840 | tf_op jit(solution)/shard_map/reduce_scatter | solution.py:100
  51.9 1.0 copy-start.3
  52.0 579.1 %all-gather.2.cloned.1.call-start = ((), (), s32[]{:S(2)}) async-start(), calls=%async_computation.3 | async-start | bytes 1064960 | tf_op jit(solution)/shard_map/all_gather | solution.py:118
  53.8 427.8 %copy-start.4 = (f32[32]{0:T(128)S(1)}, f32[32]{0:T(128)}, u32[]{:S(2)}) copy-start(f32[32]{0:T(128)} %param.16) | copy-start | bytes 388
  481.5 187.9 %reduce-scatter.5.cloned.1.call-start = ((), (), s32[]{:S(2)}) async-start(), calls=%async_computation.4 | async-start | bytes 589824 | tf_op jit(solution)/shard_map/reduce_scatter | solution.py:138
  631.1 1.9 copy-start.1
  633.4 1.2 copy-start.2
Sparse Core Ops, SparseCore 0:
  52.1 425.6 reduce-scatter.2
  482.9 148.1 all-gather.1
  636.9 32.5 reduce-scatter.4
where the time goes:
time: 678 us
  waiting for transfers between devices  603 us (89%)
  other arithmetic  25.4 us (4%)
  local copies, waits for them, and re-layouts  23.1 us (3%)
  between operations  14.6 us (2%)
  matrix products  10.6 us (2%)
    reduce_scatter x1, waiting for transfers between devices, local(): lax.psum_scatter(forward_x(packed, part_cos, part_sin), 'slab', scatter_d...  423 us
    all_gather x1, waiting for transfers between devices, local(): lax.all_gather(mixed, 'slab', axis=0, tiled=True)  148 us
    reduce_scatter x1, waiting for transfers between devices, local(): lax.psum_scatter(layer.astype(jnp.bfloat16), 'member', scatter_dimension=...  32.7 us
  transfers between devices with their start and end apart: 3, of which 3 were waited for; matrix products, arithmetic and copies ran while one was open for 0% of the time, Pallas kernels for 0%

commit v1 on v0

--- a/solution.py
+++ b/solution.py
@@ -3,8 +3,21 @@
 import jax.numpy as jnp
 from jax import lax
 from jax.sharding import PartitionSpec as P
+from jax.lax import all_to_all, axis_size
 
 TWO_PI = 2.0 * math.pi
+
+
+def define_the_stacks_all(local_x):
+    return jnp.concatenate(
+        all_to_all(
+            jnp.stack([local_x for _ in range(axis_size("slab"))], axis=0),
+            concat_axis=0,
+            axis_name="slab",
+            split_axis=0,
+        ),
+        axis=0,
+    )
 
 
 def phases(frequency, positions, length):
@@ -114,9 +127,7 @@
         .astype(jnp.bfloat16)
         .reshape(local_modes, modes_x, packed_width)
     )
-    returned = inverse_x(
-        lax.all_gather(mixed, "slab", axis=0, tiled=True), part_cos, part_sin
-    ).astype(jnp.bfloat16)
+    returned = inverse_x(define_the_stacks_all(mixed), part_cos, part_sin).astype(jnp.bfloat16)
     returned = returned.reshape(modes_y, slab_rows, 2, channels, plane_count)
     weights_y = jnp.where(jnp.arange(modes_y) == 0, 1.0, 2.0).astype(jnp.float32) / (
         length_x * length_y

time: 678 us -> 590 us (0.87)
  waiting for transfers between devices: 603 us -> 479 us
  starting transfers between devices: 0.31 us -> 36.9 us
    all_gather x1 -> x0, waiting for transfers between devices: 148 us -> none  [local(): lax.all_gather(mixed, 'slab', axis=0, tiled=True)]
    all_to_all x0 -> x1, starting transfers between devices: none -> 36.9 us  [define_the_stacks_all(): all_to_all(jnp.stack([local_x for _ in range(axis_size('slab'))], axis=0)...]
    all_to_all x0 -> x1, waiting for transfers between devices: none -> 19 us  [define_the_stacks_all(): all_to_all(jnp.stack([local_x for _ in range(axis_size('slab'))], axis=0)...]
where the time goes in v1:
time: 590 us; the launch traced here: 589 us
  waiting for transfers between devices  479 us (81%)
  starting transfers between devices  36.9 us (6%)
  other arithmetic  25.4 us (4%)
  local copies, waits for them, and re-layouts  24.1 us (4%)
  between operations  14.9 us (3%)
  matrix products  9.22 us (2%)
    reduce_scatter x1, waiting for transfers between devices, local(): lax.psum_scatter(forward_x(packed, part_cos, part_sin), 'slab', scatter_d...  425 us
    all_to_all x1, starting transfers between devices, define_the_stacks_all(): all_to_all(jnp.stack([local_x for _ in range(axis_size('slab'))], axis=0)...  36.9 us
    reduce_scatter x1, waiting for transfers between devices, local(): lax.psum_scatter(layer.astype(jnp.bfloat16), 'member', scatter_dimension=...  34.9 us
    all_to_all x1, waiting for transfers between devices, define_the_stacks_all(): all_to_all(jnp.stack([local_x for _ in range(axis_size('slab'))], axis=0)...  19 us
  transfers between devices with their start and end apart: 3, of which 3 were waited for; matrix products, arithmetic and copies ran while one was open for 0% of the time, Pallas kernels for 0%

profile of v1, /device:TPU:2, one launch (start us, length us, event | category | flops | bytes accessed | tf_op | source)
XLA Modules:
  0.0 589.1 jit_solution(3971294159763307790)
XLA Ops:
  6.5 0.0 copy-start
  6.5 0.0 reduce-scatter.3.cloned.1.call-start
  6.5 0.7 convert_element_type.79
  7.9 1.3 fusion.64
  9.2 1.3 broadcast_multiply_fusion
  10.5 1.4 multiply_convert_fusion
  12.0 0.8 fusion.4
  12.7 0.8 fusion.5
  13.5 0.1 pad_maximum_fusion.1
  13.6 0.2 copy.52
  13.8 0.2 copy.53
  14.0 0.1 pad_add_fusion
  14.1 1.9 convolution_bitcast_fusion.1
  16.0 0.6 convolution_bitcast_fusion
  16.6 5.8 reshape.102
  22.4 3.7 reshape.103
  26.1 11.8 %slice_add_fusion = (f32[64,64,1,64]{3,2,1,0:T(1,128)S(1)}, f32[64,64,1,64]{3,2,1,0:T(1,128)S(1)}) fusion(f32[64,64,2,64]{3,2,1,0:T(2,128)} %reshape.103, f32[64,64,2,64]{3,2,1,0:T(2,128)} %reshape.102), kind=kLoop, calls=%fused_computation.2 | loop fusion | flops 524288 | bytes 6291456 | tf_op jit(solution)/shard_map/add | solution.py:38
  37.9 6.8 %pad_maximum_fusion = f32[64,64,2,64]{3,2,1,0:T(2,128)} fusion(f32[64,64,1,64]{3,2,1,0:T(1,128)S(1)} %get-tuple-element.6, f32[64,64,1,64]{3,2,1,0:T(1,128)S(1)} %get-tuple-element.5), kind=kLoop, calls=%fused_computation | loop fusion | flops 524288 | bytes 4194304 | tf_op jit(solution)/shard_map/stack | solution.py:40
  44.7 7.2 %copy.55 = f32[64,64,2,64]{1,3,2,0:T(8,128)} copy(f32[64,64,2,64]{3,2,1,0:T(2,128)} %pad_maximum_fusion) | data formatting | bytes 4194304 | tf_op jit(solution)/shard_map/stack | solution.py:40
  52.0 0.0 copy-start.2
  52.0 0.0 reduce-scatter.3.cloned.1.call-update
  52.0 1.0 copy-done.2
  53.0 0.8 copy.84
  53.8 0.8 copy.82
  55.3 424.6 %reduce-scatter.3.cloned.1.call-done = f32[1,64,128]{1,2,0:T(8,128)} async-done(((f32[64,64,128]{1,2,0:T(8,128)}), f32[1,64,128]{1,2,0:T(8,128)}) %reduce-scatter.3.cloned.1.call-update) | async-done | bytes 32784 | tf_op jit(solution)/shard_map/reduce_scatter | solution.py:113
  479.8 0.8 convert_element_type.89
  480.7 0.1 copy.83
  480.8 0.1 copy.81
  480.9 0.4 fusion.18
  481.3 0.4 fusion.16
  481.7 0.4 fusion.22
  482.0 0.4 fusion.20
  482.4 0.0 copy-start.3
  482.4 0.1 copy.61
  482.5 0.1 copy.60
  482.6 0.1 copy.63
  482.7 0.1 copy.62
  482.9 0.1 copy.65
  482.9 1.3 stack.42
  484.2 36.9 %all-to-all-start = ((bf16[64,1,64,128]{3,2,1,0:T(8,128)(2,1)}), bf16[64,1,64,128]{3,2,1,0:T(8,128)(2,1)S(1)}, u32[]{:S(2)}, u32[]{:S(2)}) async-start(bf16[64,1,64,128]{3,2,1,0:T(8,128)(2,1)} %stack.42), calls=%async_computation.1 | async-start | bytes 2097152 | tf_op jit(solution)/shard_map/all_to_all | solution.py:13
  521.1 0.0 reduce-scatter.5.cloned.1.call-start
  521.2 0.0 copy-done
  521.2 0.0 copy-done.3
  521.2 1.2 fusion.2
  522.4 19.0 %all-to-all-done = bf16[64,1,64,128]{3,2,1,0:T(8,128)(2,1)S(1)} async-done(((bf16[64,1,64,128]{3,2,1,0:T(8,128)(2,1)}), bf16[64,1,64,128]{3,2,1,0:T(8,128)(2,1)S(1)}, u32[]{:S(2)}, u32[]{:S(2)}) %all-to-all-start) | async-done | bytes 1048608 | tf_op jit(solution)/shard_map/all_to_all | solution.py:13
  541.5 0.3 convolution_bitcast_fusion.3
  541.8 0.3 copy.79
  542.1 0.4 convolution_bitcast_fusion.2
  542.4 0.0 copy-start.1
  542.4 0.3 copy.80
  542.7 0.1 fusion.25
  542.8 0.1 pad_maximum_fusion.2
  542.9 0.8 fusion.29
  543.6 0.0 copy-done.1
  543.7 1.0 fusion.13
  544.7 1.1 copy.72
  545.8 0.0 reduce-scatter.5.cloned.1.call-update
  545.8 34.9 %reduce-scatter.5.cloned.1.call-done = bf16[4,8,2,512]{3,1,2,0:T(8,128)(2,1)} async-done(((bf16[32,8,2,512]{3,1,2,0:T(8,128)(2,1)}), bf16[4,8,2,512]{3,1,2,0:T(8,128)(2,1)}) %reduce-scatter.5.cloned.1.call-update) | async-done | bytes 65552 | tf_op jit(solution)/shard_map/reduce_scatter | solution.py:149
  580.7 0.9 multiply_convert_fusion.1
  581.6 0.7 copy.73
  (10 shorter events, 0.2 us)
Async XLA Ops:
  6.5 514.6 %copy-start = (bf16[32,32]{1,0:T(8,128)(2,1)S(1)}, bf16[32,32]{1,0:T(8,128)(2,1)}, u32[]{:S(2)}) copy-start(bf16[32,32]{1,0:T(8,128)(2,1)} %param.15) | copy-start | bytes 6148
  6.5 473.3 %reduce-scatter.3.cloned.1.call-start = ((), (), s32[]{:S(2)}) async-start(), calls=%async_computation.3 | async-start | bytes 4259840 | tf_op jit(solution)/shard_map/reduce_scatter | solution.py:113
  52.0 1.0 copy-start.2
  482.4 38.8 %copy-start.3 = (f32[32]{0:T(128)S(1)}, f32[32]{0:T(128)}, u32[]{:S(2)}) copy-start(f32[32]{0:T(128)} %param.16) | copy-start | bytes 388
  484.2 57.2 %all-to-all-start = ((bf16[64,1,64,128]{3,2,1,0:T(8,128)(2,1)}), bf16[64,1,64,128]{3,2,1,0:T(8,128)(2,1)S(1)}, u32[]{:S(2)}, u32[]{:S(2)}) async-start(bf16[64,1,64,128]{3,2,1,0:T(8,128)(2,1)} %stack.42), calls=%async_computation.1 | async-start | bytes 2097152 | tf_op jit(solution)/shard_map/all_to_all | solution.py:13
  521.1 59.6 %reduce-scatter.5.cloned.1.call-start = ((), (), s32[]{:S(2)}) async-start(), calls=%async_computation.4 | async-start | bytes 589824 | tf_op jit(solution)/shard_map/reduce_scatter | solution.py:149
  542.4 1.2 copy-start.1
Sparse Core Ops, SparseCore 0:
  52.1 427.6 reduce-scatter.2
  545.9 34.7 reduce-scatter.4
